TPU v7x, 512 devices: a whole 4x8x8 slice. The times are simulated.
512 devices in a mesh: blk: 32 (over x_lo, y, core), tm: 16 (over z, x_hi).
Axes of the slice: x: 4 (x_hi: 2, x_lo: 2; x = x_hi * 2 + x_lo), y: 8, z: 8, core: 2. Of those that a mesh axis runs over, the one named last changes fastest.
Arguments:
- clips: bfloat16 [32, 32, 16, 36, 256], P('blk', 'tm'), may hold values from -6 to 6
- cotangent: bfloat16 [32, 32, 16, 36, 256], P('blk', 'tm'), may hold values from -6 to 6
- conv_master: float32 [3072, 256], P('blk'), may hold values from -0.125 to 0.125
- first_moment: float32 [3072, 256], P('blk'), may hold values from -3 to 3
- second_moment: float32 [3072, 256], P('blk'), may hold values from 0.1 to 100
- norm_gain: float32 [256], replicated, may hold values from 0.5 to 1.5
- norm_bias: float32 [256], replicated, may hold values from -3 to 3
Outputs:
- block_out: bfloat16 [32, 32, 16, 36, 256], P('blk', 'tm')
- input_grad: bfloat16 [32, 32, 16, 36, 256], P('blk', 'tm')
- new_master: float32 [3072, 256], P('blk')
- new_first: float32 [3072, 256], P('blk')
- new_second: float32 [3072, 256], P('blk')
- norm_grads: float32 [2, 256], replicated
All inputs are finite; a program needn't handle non-finite values.
Results may differ from a plain program's by a relative error of at most 0.0063.
Values may be sent and summed in bfloat16 or wider, within the bound.
A program may use at most 64 MiB of HBM per device.

v0:
```python
import jax
import jax.numpy as jnp
from jax import lax
from jax.sharding import PartitionSpec as P

GROUPS = 32
beta_one = 0.9
beta_two = 0.999
learn_rate = 0.003
adam_eps = 1e-08
bias_first = 1.0 - 0.9**10
bias_second = 1.0 - 0.999**10


def extended(block, sides, width):
    for axis, dim in sides:
        count = lax.axis_size(axis)
        forward = [(i, i + 1) for i in range(count - 1)]
        backward = [(target, source) for source, target in forward]
        low = lax.ppermute(
            lax.slice_in_dim(block, block.shape[dim] - width, None, axis=dim), axis, forward
        )
        high = lax.ppermute(lax.slice_in_dim(block, 0, width, axis=dim), axis, backward)
        block = jnp.concatenate([low, block, high], axis=dim)
    return block


def norm_act(field, gain, bias):
    shape = field.shape
    grouped = field.reshape(shape[:-3] + (shape[-3] * shape[-2], GROUPS, shape[-1] // GROUPS))
    center = jnp.mean(grouped, axis=(-3, -1), keepdims=True)
    spread = jnp.mean((grouped - center) ** 2, axis=(-3, -1), keepdims=True)
    normed = ((grouped - center) * lax.rsqrt(spread + 1e-05)).reshape(shape)
    return jax.nn.silu(normed * gain + bias)


def adam_update(gradient, master, first, second):
    new_first = beta_one * first + (1.0 - beta_one) * gradient
    new_second = beta_two * second + (1.0 - beta_two) * gradient * gradient
    update = new_first / bias_first / (jnp.sqrt(new_second / bias_second) + adam_eps)
    return (master - learn_rate * update, new_first, new_second)


def shards(clips, cotangent, conv_master, first_moment, second_moment, norm_gain, norm_bias):
    f32 = jnp.float32
    frames, height, width, channels = (
        clips.shape[1],
        clips.shape[2],
        clips.shape[3],
        clips.shape[4],
    )
    weights = lax.all_gather(conv_master.astype(jnp.bfloat16), "blk", axis=0, tiled=True)
    inputs32 = clips.astype(f32)
    act32, pullback = jax.vjp(norm_act, inputs32, norm_gain, norm_bias)
    act = act32.astype(jnp.bfloat16)
    act_padded = jnp.pad(act, ((0, 0), (0, 0), (1, 1), (1, 1), (0, 0)))
    space32 = jnp.zeros(clips.shape, f32)
    for row_tap in range(3):
        for col_tap in range(3):
            tap_index = 3 * row_tap + col_tap
            window = act_padded[:, :, row_tap : row_tap + height, col_tap : col_tap + width, :]
            tap = weights[tap_index * channels : (tap_index + 1) * channels]
            space32 = space32 + jnp.einsum(
                "bfhwc,cd->bfhwd", window, tap, preferred_element_type=f32
            )
    space = space32.astype(jnp.bfloat16)
    space_padded = extended(space, (("tm", 1),), 1)
    temporal = jnp.zeros(clips.shape, f32)
    for frame_tap in range(3):
        tap = weights[(9 + frame_tap) * channels : (10 + frame_tap) * channels]
        temporal = temporal + jnp.einsum(
            "bfhwc,cd->bfhwd",
            space_padded[:, frame_tap : frame_tap + frames],
            tap,
            preferred_element_type=f32,
        )
    block_out = (inputs32 + temporal).astype(jnp.bfloat16)
    back_weights = lax.all_gather(conv_master.astype(jnp.bfloat16), "blk", axis=0, tiled=True)
    grad_padded = extended(cotangent, (("tm", 1),), 1)
    space_grad32 = jnp.zeros(clips.shape, f32)
    temporal_grads = []
    for frame_tap in range(3):
        tap = back_weights[(9 + frame_tap) * channels : (10 + frame_tap) * channels]
        space_grad32 = space_grad32 + jnp.einsum(
            "bfhwd,cd->bfhwc",
            grad_padded[:, 2 - frame_tap : 2 - frame_tap + frames],
            tap,
            preferred_element_type=f32,
        )
        temporal_grads.append(
            jnp.einsum(
                "bfhwc,bfhwd->cd",
                space_padded[:, frame_tap : frame_tap + frames],
                cotangent,
                preferred_element_type=f32,
            )
        )
    space_grad = space_grad32.astype(jnp.bfloat16)
    sgrad_padded = jnp.pad(space_grad, ((0, 0), (0, 0), (1, 1), (1, 1), (0, 0)))
    act_grad = jnp.zeros(clips.shape, f32)
    spatial_grads = []
    for row_tap in range(3):
        for col_tap in range(3):
            tap_index = 3 * row_tap + col_tap
            tap = back_weights[tap_index * channels : (tap_index + 1) * channels]
            window = act_padded[:, :, row_tap : row_tap + height, col_tap : col_tap + width, :]
            spatial_grads.append(
                jnp.einsum("bfhwc,bfhwd->cd", window, space_grad, preferred_element_type=f32)
            )
            back_window = sgrad_padded[
                :, :, 2 - row_tap : 2 - row_tap + height, 2 - col_tap : 2 - col_tap + width, :
            ]
            act_grad = act_grad + jnp.einsum(
                "bfhwd,cd->bfhwc", back_window, tap, preferred_element_type=f32
            )
    input_term, gain_grad, bias_grad = pullback(act_grad)
    input_grad = (cotangent.astype(f32) + input_term).astype(jnp.bfloat16)
    local_gradient = jnp.concatenate(spatial_grads + temporal_grads, axis=0)
    norm_grads = lax.psum(jnp.stack([gain_grad, bias_grad]), ("blk", "tm"))
    row_block = lax.psum_scatter(local_gradient, "blk", scatter_dimension=0, tiled=True)
    gradient = lax.psum(row_block, "tm")
    new_master, new_first, new_second = adam_update(
        gradient, conv_master, first_moment, second_moment
    )
    return (block_out, input_grad, new_master, new_first, new_second, norm_grads)


def solution(mesh):
    placed = (
        P("blk", "tm", None, None, None),
        P("blk", "tm", None, None, None),
        P("blk", None),
        P("blk", None),
        P("blk", None),
        P(),
        P(),
    )
    return jax.shard_map(
        shards,
        mesh=mesh,
        in_specs=placed,
        out_specs=(
            P("blk", "tm", None, None, None),
            P("blk", "tm", None, None, None),
            P("blk", None),
            P("blk", None),
            P("blk", None),
            P(),
        ),
        check_vma=False,
    )
```

profile of v0, /device:TPU:8, one launch (start us, length us, event | category | flops | bytes accessed | tf_op | source)
XLA Modules:
  0.0 426.8 jit_solution(4757618439813596500)
XLA Ops:
  7.2 1.5 convert_element_type.38
  8.8 1.3 copy.26
  10.9 4.9 %collective-permute-start.3 = (bf16[1,1,16,36,256]{4,3,2,1,0:T(8,128)(2,1)S(1)}, bf16[1,1,16,36,256]{4,3,2,1,0:T(8,128)(2,1)S(1)}, u32[]{:S(2)}, u32[]{:S(2)}) collective-permute-start(bf16[1,1,16,36,256]{4,3,2,1,0:T(8,128)(2,1)S(1)} %get-tuple-element.25), channel_id=1, source_target_pairs={{0,1},{1,2},{2,3},{3,4},{4,5},{5,6},{6,7},{7,8},{8,9},{9,10},{10,1... | collective-permute-start | bytes 884744 | tf_op jit(solution)/shard_map/ppermute | solution.py:20
  15.8 1.3 collective-permute-start.2
  18.3 11.4 %collective-permute-done.3 = bf16[1,1,16,36,256]{4,3,2,1,0:T(8,128)(2,1)S(1)} collective-permute-done((bf16[1,1,16,36,256]{4,3,2,1,0:T(8,128)(2,1)S(1)}, bf16[1,1,16,36,256]{4,3,2,1,0:T(8,128)(2,1)S(1)}, u32[]{:S(2)}, u32[]{:S(2)}) %collective-permute-start.3) | collective-permute-done | bytes 294944 | tf_op jit(solution)/shard_map/ppermute | solution.py:20
  30.5 50.4 %all-gather.2.cloned.1.call-done = bf16[3072,256]{1,0:T(8,128)(2,1)} async-done(((bf16[96,256]{1,0:T(8,128)(2,1)}), bf16[3072,256]{1,0:T(8,128)(2,1)}) %all-gather.2.cloned.1.call-update) | async-done | bytes 1572880 | tf_op jit(solution)/shard_map/all_gather | solution.py:52
  80.9 1.5 fusion.51
  82.9 1.4 fusion.9
  87.8 1.2 fusion.26
  91.7 3.0 fusion.14
  106.0 5.0 %collective-permute-start = (bf16[1,1,16,36,256]{4,3,2,1,0:T(8,128)(2,1)S(1)}, bf16[1,1,16,36,256]{4,3,2,1,0:T(8,128)(2,1)S(1)}, u32[]{:S(2)}, u32[]{:S(2)}) collective-permute-start(bf16[1,1,16,36,256]{4,3,2,1,0:T(8,128)(2,1)S(1)} %get-tuple-element.26), channel_id=1, source_target_pairs={{0,1},{1,2},{2,3},{3,4},{4,5},{5,6},{6,7},{7,8},{8,9},{9,10},{10,1... | collective-permute-start | bytes 884744 | tf_op jit(solution)/shard_map/ppermute | solution.py:20
  112.1 1.4 collective-permute-start.1
  113.5 1.1 fusion.41
  114.6 10.7 %collective-permute-done = bf16[1,1,16,36,256]{4,3,2,1,0:T(8,128)(2,1)S(1)} collective-permute-done((bf16[1,1,16,36,256]{4,3,2,1,0:T(8,128)(2,1)S(1)}, bf16[1,1,16,36,256]{4,3,2,1,0:T(8,128)(2,1)S(1)}, u32[]{:S(2)}, u32[]{:S(2)}) %collective-permute-start) | collective-permute-done | bytes 294944 | tf_op jit(solution)/shard_map/ppermute | solution.py:20
  125.3 1.2 fusion.40
  126.5 1.1 fusion.39
  128.4 1.2 fusion.38
  131.7 98.4 %psum.15 = f32[2,256]{1,0:T(2,128)} all-reduce(f32[2,256]{1,0:T(2,128)S(1)} %pad_maximum_fusion.4), channel_id=1, replica_groups=mesh['blk'=32,'tm'=16] {'blk','tm'}, use_global_device_ids=true, to_apply=%region_14.15 | all-reduce | flops 512 | bytes 4096 | tf_op jit(solution)/shard_map/psum | solution.py:119
  230.1 1.4 fusion.129
  231.6 1.4 fusion.127
  233.0 19.1 %reduce-scatter.2.cloned.1.call-done = f32[96,256]{1,0:T(8,128)} async-done(((f32[3072,256]{1,0:T(8,128)}), f32[96,256]{1,0:T(8,128)}) %reduce-scatter.2.cloned.1.call-update) | async-done | bytes 98320 | tf_op jit(solution)/shard_map/reduce_scatter | solution.py:120
  252.1 2.2 fusion.11
  255.3 163.4 %all-reduce.4.cloned.1.call-done = f32[96,256]{1,0:T(8,128)} async-done(((f32[96,256]{1,0:T(8,128)}), f32[96,256]{1,0:T(8,128)}) %all-reduce.4.cloned.1.call-update) | async-done | bytes 98320 | tf_op jit(solution)/shard_map/psum | solution.py:121
  418.7 1.6 multiply_subtract_fusion
  (99 shorter events, 25.4 us)
Async XLA Ops:
  7.2 73.8 %all-gather.2.cloned.1.call-start = ((), (), s32[]{:S(2)}) async-start(), calls=%async_computation.1 | async-start | bytes 1622016 | tf_op jit(solution)/shard_map/all_gather | solution.py:52
  8.7 8.4 %copy-start = (bf16[1,2,16,36,256]{4,2,3,1,0:T(8,128)(2,1)S(1)}, bf16[1,2,16,36,256]{4,2,3,1,0:T(8,128)(2,1)}, u32[]{:S(2)}) copy-start(bf16[1,2,16,36,256]{4,2,3,1,0:T(8,128)(2,1)} %param.7) | copy-start | bytes 1769476
  8.8 243.3 %reduce-scatter.2.cloned.1.call-start = ((), (), s32[]{:S(2)}) async-start(), calls=%async_computation.2 | async-start | bytes 3244032 | tf_op jit(solution)/shard_map/reduce_scatter | solution.py:120
  10.9 18.9 %collective-permute-start.3 = (bf16[1,1,16,36,256]{4,3,2,1,0:T(8,128)(2,1)S(1)}, bf16[1,1,16,36,256]{4,3,2,1,0:T(8,128)(2,1)S(1)}, u32[]{:S(2)}, u32[]{:S(2)}) collective-permute-start(bf16[1,1,16,36,256]{4,3,2,1,0:T(8,128)(2,1)S(1)} %get-tuple-element.25), channel_id=1, source_target_pairs={{0,1},{1,2},{2,3},{3,4},{4,5},{5,6},{6,7},{7,8},{8,9},{9,10},{10,1... | collective-permute-start | bytes 884744 | tf_op jit(solution)/shard_map/ppermute | solution.py:20
  15.8 67.1 %collective-permute-start.2 = (bf16[1,1,16,36,256]{4,3,2,1,0:T(8,128)(2,1)}, bf16[1,1,16,36,256]{4,3,2,1,0:T(8,128)(2,1)}, u32[]{:S(2)}, u32[]{:S(2)}) collective-permute-start(bf16[1,1,16,36,256]{4,3,2,1,0:T(8,128)(2,1)} %get-tuple-element.24), channel_id=1, source_target_pairs={{1,0},{2,1},{3,2},{4,3},{5,4},{6,5},{7,6},{8,7},{9,8},{10,9},{11,1... | collective-permute-start | bytes 884744 | tf_op jit(solution)/shard_map/ppermute | solution.py:23
  17.9 64.5 %copy-start.2 = (bf16[1,2,16,36,256]{4,2,3,1,0:T(8,128)(2,1)S(1)}, bf16[1,2,16,36,256]{4,2,3,1,0:T(8,128)(2,1)}, u32[]{:S(2)}) copy-start(bf16[1,2,16,36,256]{4,2,3,1,0:T(8,128)(2,1)} %param.8) | copy-start | bytes 1769476
  29.8 0.7 copy-start.12
  80.9 1.6 copy-start.1
  87.1 0.7 copy-start.15
  87.1 0.7 copy-start.16
  89.0 1.1 copy-start.5
  90.1 1.7 copy-start.3
  106.0 19.3 %collective-permute-start = (bf16[1,1,16,36,256]{4,3,2,1,0:T(8,128)(2,1)S(1)}, bf16[1,1,16,36,256]{4,3,2,1,0:T(8,128)(2,1)S(1)}, u32[]{:S(2)}, u32[]{:S(2)}) collective-permute-start(bf16[1,1,16,36,256]{4,3,2,1,0:T(8,128)(2,1)S(1)} %get-tuple-element.26), channel_id=1, source_target_pairs={{0,1},{1,2},{2,3},{3,4},{4,5},{5,6},{6,7},{7,8},{8,9},{9,10},{10,1... | collective-permute-start | bytes 884744 | tf_op jit(solution)/shard_map/ppermute | solution.py:20
  112.1 13.3 %copy-start.4 = (bf16[1,2,16,36,256]{4,2,3,1,0:T(8,128)(2,1)S(1)}, bf16[1,2,16,36,256]{4,2,3,1,0:T(8,128)(2,1)}, u32[]{:S(2)}) copy-start(bf16[1,2,16,36,256]{4,2,3,1,0:T(8,128)(2,1)} %param.8) | copy-start | bytes 1769476
  112.1 15.6 %collective-permute-start.1 = (bf16[1,1,16,36,256]{4,3,2,1,0:T(8,128)(2,1)S(1)}, bf16[1,1,16,36,256]{4,3,2,1,0:T(8,128)(2,1)S(1)}, u32[]{:S(2)}, u32[]{:S(2)}) collective-permute-start(bf16[1,1,16,36,256]{4,3,2,1,0:T(8,128)(2,1)S(1)} %get-tuple-element.27), channel_id=1, source_target_pairs={{1,0},{2,1},{3,2},{4,3},{5,4},{6,5},{7,6},{8,7},{9,8},{10,9},{11,1... | collective-permute-start | bytes 884744 | tf_op jit(solution)/shard_map/ppermute | solution.py:23
  125.3 1.2 copy-start.8
  127.7 0.7 copy-start.10
  129.7 1.1 copy-start.6
  129.7 289.0 %all-reduce.4.cloned.1.call-start = ((), (), s32[]{:S(2)}) async-start(), calls=%async_computation.3 | async-start | bytes 196608 | tf_op jit(solution)/shard_map/psum | solution.py:121
  131.7 99.9 %copy-start.11 = (bf16[1,1,16,36,256]{4,3,2,1,0:T(8,128)(2,1)S(1)}, bf16[1,1,16,36,256]{4,3,2,1,0:T(8,128)(2,1)}, u32[]{:S(2)}) copy-start(bf16[1,1,16,36,256]{4,3,2,1,0:T(8,128)(2,1)} %copy-done.10) | copy-start | bytes 884740
  231.6 20.5 %copy-start.9 = (bf16[1,1,16,36,256]{4,3,2,1,0:T(8,128)(2,1)S(1)}, bf16[1,1,16,36,256]{4,3,2,1,0:T(8,128)(2,1)}, u32[]{:S(2)}) copy-start(bf16[1,1,16,36,256]{4,3,2,1,0:T(8,128)(2,1)} %copy-done.8) | copy-start | bytes 884740
  254.3 164.3 %copy-start.7 = (f32[96,256]{1,0:T(8,128)S(1)}, f32[96,256]{1,0:T(8,128)}, u32[]{:S(2)}) copy-start(f32[96,256]{1,0:T(8,128)} %param.9) | copy-start | bytes 294916
  254.3 164.3 %copy-start.13 = (f32[96,256]{1,0:T(8,128)S(1)}, f32[96,256]{1,0:T(8,128)}, u32[]{:S(2)}) copy-start(f32[96,256]{1,0:T(8,128)} %param.10) | copy-start | bytes 294916
  254.4 164.3 %copy-start.14 = (f32[96,256]{1,0:T(8,128)S(1)}, f32[96,256]{1,0:T(8,128)}, u32[]{:S(2)}) copy-start(f32[96,256]{1,0:T(8,128)} %param.11) | copy-start | bytes 294916
Sparse Core Ops, SparseCore 0:
  10.7 70.1 all-gather.1
  129.8 122.2 reduce-scatter.1
  255.0 163.6 all-reduce.3
where the time goes:
time: 427 us
  waiting for transfers between devices  255 us (60%)
  blocking collectives  98.4 us (23%)
  matrix products  29.6 us (7%)
  between operations  14.1 us (3%)
  starting transfers between devices  12.7 us (3%)
  local copies, waits for them, and re-layouts  9.06 us (2%)
  other arithmetic  7.8 us (2%)
    psum x1, waiting for transfers between devices, shards(): gradient = lax.psum(row_block, 'tm')  163 us
    psum x1, blocking collectives, shards(): norm_grads = lax.psum(jnp.stack([gain_grad, bias_grad]), ('blk', 'tm'))  98.4 us
    all_gather x1, waiting for transfers between devices, shards(): lax.all_gather(conv_master.astype(jnp.bfloat16), 'blk', axis=0, tiled=True)  50.4 us
    ppermute x2, waiting for transfers between devices, extended(): lax.ppermute(lax.slice_in_dim(block, block.shape[dim] - width, None, axis...  22.2 us
    reduce_scatter x1, waiting for transfers between devices, shards(): lax.psum_scatter(local_gradient, 'blk', scatter_dimension=0, tiled=True)  19.1 us
    ppermute x2, starting transfers between devices, extended(): lax.ppermute(lax.slice_in_dim(block, block.shape[dim] - width, None, axis...  9.9 us
    dot_general x9, matrix products, shards(): jnp.einsum('bfhwc,bfhwd->cd', window, space_grad, preferred_element_type=...  9.86 us
  transfers between devices with their start and end apart: 7, of which 5 were waited for; matrix products, arithmetic and copies ran while one was open for 4% of the time, Pallas kernels for 0%

commit v1 on v0

--- a/solution.py
+++ b/solution.py
@@ -49,7 +49,14 @@
         clips.shape[3],
         clips.shape[4],
     )
-    weights = lax.all_gather(conv_master.astype(jnp.bfloat16), "blk", axis=0, tiled=True)
+    m = conv_master.astype(jnp.bfloat16)
+    opened = lax.all_to_all(
+        jnp.stack(tuple((m for _ in range(lax.axis_size("blk")))), axis=0),
+        axis_name="blk",
+        split_axis=0,
+        concat_axis=0,
+    )
+    weights = jnp.concatenate(opened, axis=0)
     inputs32 = clips.astype(f32)
     act32, pullback = jax.vjp(norm_act, inputs32, norm_gain, norm_bias)
     act = act32.astype(jnp.bfloat16)

time: 427 us -> 442 us (1.035)
  matrix products: 29.6 us -> 38.6 us
  starting transfers between devices: 12.7 us -> 20.6 us
    dot_general x9, matrix products: 3.51 us -> 11.6 us  [shards(): jnp.einsum('bfhwc,cd->bfhwd', window, tap, preferred_element_type=f32)]
    all_to_all x0 -> x1, starting transfers between devices: none -> 7.91 us  [shards(): lax.all_to_all(jnp.stack(tuple((m for _ in range(lax.axis_size('blk')))),...]
    ppermute x2, waiting for transfers between devices: 22.2 us -> 14.7 us  [extended(): lax.ppermute(lax.slice_in_dim(block, block.shape[dim] - width, None, axis...]
    all_gather x1, waiting for transfers between devices: 50.4 us -> 56.7 us  [shards(): lax.all_gather(conv_master.astype(jnp.bfloat16), 'blk', axis=0, tiled=True)]
  transfers between devices with their start and end apart: 7 -> 8, of which waited for: 5 -> 5; matrix products, arithmetic and copies ran while one was open for 4% -> 8% of each run, Pallas kernels for 0% -> 0%
where the time goes in v1:
time: 442 us
  waiting for transfers between devices  251 us (57%)
  blocking collectives  101 us (23%)
  matrix products  38.6 us (9%)
  starting transfers between devices  20.6 us (5%)
  between operations  14.1 us (3%)
  local copies, waits for them, and re-layouts  8.91 us (2%)
  other arithmetic  7.82 us (2%)
    psum x1, waiting for transfers between devices, shards(): gradient = lax.psum(row_block, 'tm')  164 us
    psum x1, blocking collectives, shards(): norm_grads = lax.psum(jnp.stack([gain_grad, bias_grad]), ('blk', 'tm'))  101 us
    all_gather x1, waiting for transfers between devices, shards(): lax.all_gather(conv_master.astype(jnp.bfloat16), 'blk', axis=0, tiled=True)  56.7 us
    reduce_scatter x1, waiting for transfers between devices, shards(): lax.psum_scatter(local_gradient, 'blk', scatter_dimension=0, tiled=True)  15.8 us
    ppermute x2, waiting for transfers between devices, extended(): lax.ppermute(lax.slice_in_dim(block, block.shape[dim] - width, None, axis...  14.7 us
    dot_general x9, matrix products, shards(): jnp.einsum('bfhwc,cd->bfhwd', window, tap, preferred_element_type=f32)  11.6 us
    ppermute x2, starting transfers between devices, extended(): lax.ppermute(lax.slice_in_dim(block, block.shape[dim] - width, None, axis...  10 us
    dot_general x9, matrix products, shards(): jnp.einsum('bfhwc,bfhwd->cd', window, space_grad, preferred_element_type=...  9.84 us
  transfers between devices with their start and end apart: 8, of which 5 were waited for; matrix products, arithmetic and copies ran while one was open for 8% of the time, Pallas kernels for 0%

profile of v1, /device:TPU:8, one launch (start us, length us, event | category | flops | bytes accessed | tf_op | source)
XLA Modules:
  0.0 441.5 jit_solution(12793911782159635749)
XLA Ops:
  7.2 1.5 convert_element_type.38
  10.1 4.9 %collective-permute-start.3 = (bf16[1,1,16,36,256]{4,3,2,1,0:T(8,128)(2,1)S(1)}, bf16[1,1,16,36,256]{4,3,2,1,0:T(8,128)(2,1)S(1)}, u32[]{:S(2)}, u32[]{:S(2)}) collective-permute-start(bf16[1,1,16,36,256]{4,3,2,1,0:T(8,128)(2,1)S(1)} %get-tuple-element.25), channel_id=1, source_target_pairs={{0,1},{1,2},{2,3},{3,4},{4,5},{5,6},{6,7},{7,8},{8,9},{9,10},{10,1... | collective-permute-start | bytes 884744 | tf_op jit(solution)/shard_map/ppermute | solution.py:20
  15.0 1.3 collective-permute-start.2
  16.3 1.4 stack.8
  17.7 7.9 %all-to-all-start = ((bf16[32,96,256]{2,1,0:T(8,128)(2,1)}), bf16[32,96,256]{2,1,0:T(8,128)(2,1)}, u32[]{:S(2)}, u32[]{:S(2)}) async-start(bf16[32,96,256]{2,1,0:T(8,128)(2,1)} %stack.8), calls=%async_computation | async-start | bytes 3145728 | tf_op jit(solution)/shard_map/all_to_all | solution.py:53
  26.9 3.9 collective-permute-done.3
  30.8 56.7 %all-gather.2.cloned.1.call-done = bf16[3072,256]{1,0:T(8,128)(2,1)} async-done(((bf16[96,256]{1,0:T(8,128)(2,1)}), bf16[3072,256]{1,0:T(8,128)(2,1)}) %all-gather.2.cloned.1.call-update) | async-done | bytes 1572880 | tf_op jit(solution)/shard_map/all_gather | solution.py:85
  87.5 1.4 fusion.51
  97.2 3.0 fusion.14
  111.7 1.3 convolution_add_fusion.15
  114.2 1.3 convolution_add_fusion.13
  115.5 1.3 convolution_add_fusion.12
  116.8 1.4 convolution_add_fusion.11
  118.2 1.3 fusion.10
  119.6 5.1 %collective-permute-start = (bf16[1,1,16,36,256]{4,3,2,1,0:T(8,128)(2,1)S(1)}, bf16[1,1,16,36,256]{4,3,2,1,0:T(8,128)(2,1)S(1)}, u32[]{:S(2)}, u32[]{:S(2)}) collective-permute-start(bf16[1,1,16,36,256]{4,3,2,1,0:T(8,128)(2,1)S(1)} %get-tuple-element.26), channel_id=1, source_target_pairs={{0,1},{1,2},{2,3},{3,4},{4,5},{5,6},{6,7},{7,8},{8,9},{9,10},{10,1... | collective-permute-start | bytes 884744 | tf_op jit(solution)/shard_map/ppermute | solution.py:20
  125.7 1.3 collective-permute-start.1
  128.1 10.8 %collective-permute-done = bf16[1,1,16,36,256]{4,3,2,1,0:T(8,128)(2,1)S(1)} collective-permute-done((bf16[1,1,16,36,256]{4,3,2,1,0:T(8,128)(2,1)S(1)}, bf16[1,1,16,36,256]{4,3,2,1,0:T(8,128)(2,1)S(1)}, u32[]{:S(2)}, u32[]{:S(2)}) %collective-permute-start) | collective-permute-done | bytes 294944 | tf_op jit(solution)/shard_map/ppermute | solution.py:20
  145.3 100.5 %psum.15 = f32[2,256]{1,0:T(2,128)} all-reduce(f32[2,256]{1,0:T(2,128)S(1)} %pad_maximum_fusion.4), channel_id=1, replica_groups=mesh['blk'=32,'tm'=16] {'blk','tm'}, use_global_device_ids=true, to_apply=%region_14.15 | all-reduce | flops 512 | bytes 4096 | tf_op jit(solution)/shard_map/psum | solution.py:126
  245.8 2.4 fusion.129
  248.2 2.4 fusion.127
  250.6 15.8 %reduce-scatter.2.cloned.1.call-done = f32[96,256]{1,0:T(8,128)} async-done(((f32[3072,256]{1,0:T(8,128)}), f32[96,256]{1,0:T(8,128)}) %reduce-scatter.2.cloned.1.call-update) | async-done | bytes 98320 | tf_op jit(solution)/shard_map/reduce_scatter | solution.py:127
  266.4 2.3 fusion.11
  269.6 163.8 %all-reduce.4.cloned.1.call-done = f32[96,256]{1,0:T(8,128)} async-done(((f32[96,256]{1,0:T(8,128)}), f32[96,256]{1,0:T(8,128)}) %all-reduce.4.cloned.1.call-update) | async-done | bytes 98320 | tf_op jit(solution)/shard_map/psum | solution.py:128
  433.4 1.6 multiply_subtract_fusion
  (94 shorter events, 33.0 us)
Async XLA Ops:
  7.2 80.3 %all-gather.2.cloned.1.call-start = ((), (), s32[]{:S(2)}) async-start(), calls=%async_computation.2 | async-start | bytes 1622016 | tf_op jit(solution)/shard_map/all_gather | solution.py:85
  8.7 7.6 %copy-start.5 = (bf16[96,256]{1,0:T(8,128)(2,1)S(1)}, bf16[96,256]{1,0:T(8,128)(2,1)}, u32[]{:S(2)}) copy-start(bf16[96,256]{1,0:T(8,128)(2,1)} %convert_element_type.38) | copy-start | bytes 147460
  10.1 20.7 %collective-permute-start.3 = (bf16[1,1,16,36,256]{4,3,2,1,0:T(8,128)(2,1)S(1)}, bf16[1,1,16,36,256]{4,3,2,1,0:T(8,128)(2,1)S(1)}, u32[]{:S(2)}, u32[]{:S(2)}) collective-permute-start(bf16[1,1,16,36,256]{4,3,2,1,0:T(8,128)(2,1)S(1)} %get-tuple-element.25), channel_id=1, source_target_pairs={{0,1},{1,2},{2,3},{3,4},{4,5},{5,6},{6,7},{7,8},{8,9},{9,10},{10,1... | collective-permute-start | bytes 884744 | tf_op jit(solution)/shard_map/ppermute | solution.py:20
  15.0 74.3 %collective-permute-start.2 = (bf16[1,1,16,36,256]{4,3,2,1,0:T(8,128)(2,1)S(1)}, bf16[1,1,16,36,256]{4,3,2,1,0:T(8,128)(2,1)S(1)}, u32[]{:S(2)}, u32[]{:S(2)}) collective-permute-start(bf16[1,1,16,36,256]{4,3,2,1,0:T(8,128)(2,1)S(1)} %get-tuple-element.24), channel_id=1, source_target_pairs={{1,0},{2,1},{3,2},{4,3},{5,4},{6,5},{7,6},{8,7},{9,8},{10,9},{11,1... | collective-permute-start | bytes 884744 | tf_op jit(solution)/shard_map/ppermute | solution.py:23
  17.7 8.0 %copy-start = (bf16[1,2,16,36,256]{4,2,3,1,0:T(8,128)(2,1)S(1)}, bf16[1,2,16,36,256]{4,2,3,1,0:T(8,128)(2,1)}, u32[]{:S(2)}) copy-start(bf16[1,2,16,36,256]{4,2,3,1,0:T(8,128)(2,1)} %param.7) | copy-start | bytes 1769476
  17.7 90.2 %all-to-all-start = ((bf16[32,96,256]{2,1,0:T(8,128)(2,1)}), bf16[32,96,256]{2,1,0:T(8,128)(2,1)}, u32[]{:S(2)}, u32[]{:S(2)}) async-start(bf16[32,96,256]{2,1,0:T(8,128)(2,1)} %stack.8), calls=%async_computation | async-start | bytes 3145728 | tf_op jit(solution)/shard_map/all_to_all | solution.py:53
  25.6 240.7 %reduce-scatter.2.cloned.1.call-start = ((), (), s32[]{:S(2)}) async-start(), calls=%async_computation.3 | async-start | bytes 3244032 | tf_op jit(solution)/shard_map/reduce_scatter | solution.py:127
  26.5 62.4 %copy-start.1 = (bf16[1,2,16,36,256]{4,2,3,1,0:T(8,128)(2,1)S(1)}, bf16[1,2,16,36,256]{4,2,3,1,0:T(8,128)(2,1)}, u32[]{:S(2)}) copy-start(bf16[1,2,16,36,256]{4,2,3,1,0:T(8,128)(2,1)} %param.8) | copy-start | bytes 1769476
  87.5 1.5 copy-start.4
  92.6 0.7 copy-start.11
  92.6 0.7 copy-start.12
  94.5 1.1 copy-start.2
  119.6 19.4 %collective-permute-start = (bf16[1,1,16,36,256]{4,3,2,1,0:T(8,128)(2,1)S(1)}, bf16[1,1,16,36,256]{4,3,2,1,0:T(8,128)(2,1)S(1)}, u32[]{:S(2)}, u32[]{:S(2)}) collective-permute-start(bf16[1,1,16,36,256]{4,3,2,1,0:T(8,128)(2,1)S(1)} %get-tuple-element.26), channel_id=1, source_target_pairs={{0,1},{1,2},{2,3},{3,4},{4,5},{5,6},{6,7},{7,8},{8,9},{9,10},{10,1... | collective-permute-start | bytes 884744 | tf_op jit(solution)/shard_map/ppermute | solution.py:20
  125.7 15.6 %collective-permute-start.1 = (bf16[1,1,16,36,256]{4,3,2,1,0:T(8,128)(2,1)S(1)}, bf16[1,1,16,36,256]{4,3,2,1,0:T(8,128)(2,1)S(1)}, u32[]{:S(2)}, u32[]{:S(2)}) collective-permute-start(bf16[1,1,16,36,256]{4,3,2,1,0:T(8,128)(2,1)S(1)} %get-tuple-element.27), channel_id=1, source_target_pairs={{1,0},{2,1},{3,2},{4,3},{5,4},{6,5},{7,6},{8,7},{9,8},{10,9},{11,1... | collective-permute-start | bytes 884744 | tf_op jit(solution)/shard_map/ppermute | solution.py:23
  141.3 0.7 copy-start.7
  143.3 1.1 copy-start.3
  143.3 290.0 %all-reduce.4.cloned.1.call-start = ((), (), s32[]{:S(2)}) async-start(), calls=%async_computation.4 | async-start | bytes 196608 | tf_op jit(solution)/shard_map/psum | solution.py:128
  145.3 102.9 %copy-start.8 = (bf16[1,1,16,36,256]{4,3,2,1,0:T(8,128)(2,1)S(1)}, bf16[1,1,16,36,256]{4,3,2,1,0:T(8,128)(2,1)}, u32[]{:S(2)}) copy-start(bf16[1,1,16,36,256]{4,3,2,1,0:T(8,128)(2,1)} %copy-done.7) | copy-start | bytes 884740
  268.6 164.7 %copy-start.6 = (f32[96,256]{1,0:T(8,128)S(1)}, f32[96,256]{1,0:T(8,128)}, u32[]{:S(2)}) copy-start(f32[96,256]{1,0:T(8,128)} %param.9) | copy-start | bytes 294916
  268.6 164.7 %copy-start.9 = (f32[96,256]{1,0:T(8,128)S(1)}, f32[96,256]{1,0:T(8,128)}, u32[]{:S(2)}) copy-start(f32[96,256]{1,0:T(8,128)} %param.10) | copy-start | bytes 294916
  268.7 164.7 %copy-start.10 = (f32[96,256]{1,0:T(8,128)S(1)}, f32[96,256]{1,0:T(8,128)}, u32[]{:S(2)}) copy-start(f32[96,256]{1,0:T(8,128)} %param.11) | copy-start | bytes 294916
Sparse Core Ops, SparseCore 0:
  10.7 76.7 all-gather.1
  143.4 122.8 reduce-scatter.1
  269.2 164.0 all-reduce.3
